TPU v7x, 32 devices: a whole 2x2x4 slice. The times are simulated.
32 devices in a mesh: grp: 2 (over y), ctx: 4 (over z), head: 4 (over x, core).
Axes of the slice: x: 2, y: 2, z: 4, core: 2. Of those that a mesh axis runs over, the one named last changes fastest.
Arguments:
- behavior_embed: bfloat16 [4, 2048, 256], P('grp', 'ctx'), parts along dimension 0, may hold values from -6 to 6
- behavior_mask: int32 [4, 2048], P('grp', 'ctx'), parts along dimension 0, may hold values 0 or 1
- history_len: int32 [4], P('grp'), parts along dimension 0, may hold values from 256 to 2048, as said below
- log_decay: float32 [8, 4, 2048], P('head', 'grp', 'ctx'), parts along dimension 1, may hold values from -2 to 0
- candidate_embed: bfloat16 [4, 512, 256], P('grp', 'ctx'), parts along dimension 0, may hold values from -6 to 6
- input_weight: bfloat16 [256, 1024], replicated, may hold values from -0.375 to 0.375
- input_gain: float32 [1024], replicated, may hold values from 0.5 to 1.5
- proj_weight: bfloat16 [4, 1024, 1024], P(None, None, 'head'), may hold values from -0.1875 to 0.1875
- output_gain: float32 [1024], P('head'), may hold values from 0.5 to 1.5
- ranker_first: bfloat16 [1024, 1024], P('head'), may hold values from -0.1875 to 0.1875
- ranker_second: bfloat16 [1024], replicated, may hold values from -0.1875 to 0.1875
Outputs:
- history_out: bfloat16 [4, 2048, 1024], P('grp', 'ctx', 'head'), parts along dimension 0
- scores: float32 [4, 512], P('grp', ('ctx', 'head')), parts along dimension 0
There are 2 independent parts, one for each index of `grp`. A program takes and returns all parts, laid end to end along the dimension named above; an argument that names none is the same for every part. Nothing has to cross between parts.
Inputs may be any that keep to these rules, and one draw needn't show every extreme that they name: Histories are padded at the start: the last history_len[u] positions hold user u's behaviors; at least one user's history fills all 2048 positions.
All inputs are finite; a program needn't handle non-finite values. No bound on the sum of `behavior_mask` on one device may be relied on, other than what follows from the above.
Results may differ from a plain program's by a relative error of at most 0.0098.
Values may be sent and summed in bfloat16 or wider, within the bound.
No kernel may reach another device: no remote copies, remote signals or barrier semaphores. Data moves between devices by JAX's collectives and lax.ppermute only.
A program may use at most 64 MiB of HBM per device.

v0:
```python
import jax
import jax.numpy as jnp
from jax import lax
from jax.sharding import PartitionSpec as P

DH = 128


epsilon = 1e-05
highest = lax.Precision.HIGHEST


def rms_norm(values, gain_row):
    mean_square = jnp.mean(values * values, axis=-1, keepdims=True)
    return values * lax.rsqrt(mean_square + epsilon) * gain_row


def local(
    behavior_embed,
    behavior_mask,
    history_len,
    log_decay,
    candidate_embed,
    input_weight,
    input_gain,
    proj_weight,
    output_gain,
    ranker_first,
    ranker_second,
):
    user_count, span_len = behavior_mask.shape
    cand_len = candidate_embed.shape[1]
    embed_width = behavior_embed.shape[2]
    head_cols = proj_weight.shape[2]
    heads_here = head_cols // DH
    ctx_count = lax.axis_size("ctx")
    ctx_index = lax.axis_index("ctx")
    head_count = lax.axis_size("head")
    head_index = lax.axis_index("head")
    seq_total = span_len * ctx_count
    position_indices = ctx_index * span_len + jnp.arange(span_len, dtype=jnp.int32)
    valid_mask = (
        (position_indices[None, :] >= seq_total - history_len[:, None]) & (behavior_mask == 1)
    ).astype(jnp.float32)
    behavior_rows = behavior_embed.reshape(user_count * span_len, embed_width)
    candidate_rows = jnp.transpose(candidate_embed, (1, 0, 2)).reshape(
        cand_len * user_count, embed_width
    )
    behavior_raw = lax.optimization_barrier(
        jnp.dot(behavior_rows, input_weight, preferred_element_type=jnp.float32).astype(
            jnp.bfloat16
        )
    )
    candidate_raw = lax.optimization_barrier(
        jnp.dot(candidate_rows, input_weight, preferred_element_type=jnp.float32).astype(
            jnp.bfloat16
        )
    )
    behavior_norm = rms_norm(behavior_raw.astype(jnp.float32), input_gain).astype(jnp.bfloat16)
    candidate_norm = rms_norm(candidate_raw.astype(jnp.float32), input_gain).astype(jnp.bfloat16)
    projected = jnp.einsum(
        "rd,pdc->prc", behavior_norm, proj_weight, preferred_element_type=jnp.float32
    )
    head_shape = (user_count, span_len, heads_here, DH)
    query_rows = projected[0].astype(jnp.bfloat16).reshape(head_shape)
    key_rows = (projected[1] * DH ** (-0.5)).astype(jnp.bfloat16).reshape(head_shape)
    value_rows = projected[2].astype(jnp.bfloat16).reshape(head_shape)
    gate_rows = projected[3].astype(jnp.bfloat16).reshape(head_shape)
    cumulative = jnp.cumsum(log_decay, axis=-1)
    span_total = cumulative[..., -1]
    row_ids = jnp.arange(span_len)
    causal = row_ids[:, None] >= row_ids[None, :]
    log_gap = cumulative[..., :, None] - cumulative[..., None, :]
    decay_matrix = (
        jnp.where(causal, jnp.exp(jnp.where(causal, log_gap, 0.0)), 0.0)
        * valid_mask[None, :, None, :]
    )
    scores_local = jnp.einsum(
        "uihd,ujhd->huij", query_rows, key_rows, preferred_element_type=jnp.float32
    )
    value_wide = value_rows.astype(jnp.float32)
    within = jnp.einsum(
        "huij,ujhd->uihd", scores_local * decay_matrix, value_wide, precision=highest
    )
    key_weight = jnp.exp(span_total[..., None] - cumulative) * valid_mask[None]
    local_state = jnp.einsum(
        "ujhd,ujhe->hude",
        key_rows.astype(jnp.float32) * jnp.transpose(key_weight, (1, 2, 0))[..., None],
        value_wide,
        precision=highest,
    )
    log_rows = lax.all_gather(span_total[None], "ctx", axis=0, tiled=True)
    through = jnp.cumsum(log_rows, axis=0)
    device_ids = jnp.arange(ctx_count)
    before_self = jnp.sum(jnp.where(device_ids[:, None, None] < ctx_index, log_rows, 0.0), axis=0)
    all_logs = jnp.sum(log_rows, axis=0)
    shard_piece = lax.all_gather(local_state[None], "ctx", axis=0, tiled=True)
    piece_len = shard_piece.shape[0]
    owners = jnp.arange(piece_len)
    weight_in = jnp.where(
        owners[:, None, None] < ctx_index,
        jnp.exp(jnp.minimum(before_self[None] - through, 0.0)),
        0.0,
    )
    weight_end = jnp.exp(jnp.minimum(all_logs[None] - through, 0.0))
    state_in = jnp.einsum("phu,phude->hude", weight_in, shard_piece, precision=highest)
    final_full = jnp.einsum("phu,phude->hude", weight_end, shard_piece, precision=highest)
    final_state = final_full.astype(jnp.bfloat16)
    carried = (
        jnp.einsum("uihd,hude->uihe", query_rows.astype(jnp.float32), state_in, precision=highest)
        * jnp.exp(jnp.transpose(cumulative, (1, 2, 0)))[..., None]
    )
    readout = within + carried
    gain_heads = output_gain.reshape(heads_here, DH)
    history_out = (
        (rms_norm(readout, gain_heads) * jax.nn.silu(gate_rows.astype(jnp.float32)))
        .reshape(user_count, span_len, head_cols)
        .astype(jnp.bfloat16)
    )
    candidate_query = (
        jnp.dot(candidate_norm, proj_weight[0], preferred_element_type=jnp.float32)
        .astype(jnp.bfloat16)
        .reshape(cand_len, user_count, heads_here, DH)
    )
    candidate_read = jnp.einsum(
        "cuhd,hude->cuhe", candidate_query, final_state, preferred_element_type=jnp.float32
    )
    own_cols = lax.dynamic_slice_in_dim(candidate_norm, head_index * head_cols, head_cols, 1)
    candidate_feat = (
        rms_norm(candidate_read, gain_heads).reshape(cand_len * user_count, head_cols)
        + own_cols.astype(jnp.float32)
    ).astype(jnp.bfloat16)
    share_rows = cand_len * user_count // head_count
    summed = lax.psum(
        jnp.dot(candidate_feat, ranker_first, preferred_element_type=jnp.float32), "head"
    )
    hidden = lax.dynamic_slice_in_dim(summed, head_index * share_rows, share_rows, 0)
    scores = jnp.dot(jax.nn.silu(hidden), ranker_second.astype(jnp.float32), precision=highest)
    scores = scores.reshape(cand_len // head_count, user_count).T
    return (history_out, scores)


def solution(mesh):
    in_specs = (
        P("grp", "ctx", None),
        P("grp", "ctx"),
        P("grp"),
        P("head", "grp", "ctx"),
        P("grp", "ctx", None),
        P(),
        P(),
        P(None, None, "head"),
        P("head"),
        P("head", None),
        P(),
    )
    out_specs = (P("grp", "ctx", "head"), P("grp", ("ctx", "head")))
    return jax.shard_map(local, mesh=mesh, in_specs=in_specs, out_specs=out_specs, check_vma=False)
```

profile of v0, /device:TPU:0, one launch (start us, length us, event | category | flops | bytes accessed | tf_op | source)
XLA Modules:
  0.0 99.1 jit_solution(13549878280901394313)
XLA Ops:
  7.2 0.0 copy-start
  7.2 0.0 copy-start.12
  7.2 0.0 all-gather.4.cloned.1.call-start
  7.3 1.0 copy-done
  8.2 1.7 %convolution_convert_fusion = bf16[1024,1024]{1,0:T(8,128)(2,1)S(1)} fusion(bf16[1024,256]{1,0:T(8,128)(2,1)S(1)} %bitcast.59, bf16[256,1024]{1,0:T(8,128)(2,1)} %param.16), kind=kOutput, calls=%fused_computation.22 | convolution fusion | flops 537919488 | bytes 3145728 | tf_op jit(solution)/shard_map/dot_general | solution.py:50
  10.0 0.5 fusion.1
  10.5 2.4 %fusion.69 = (bf16[4,1024,256]{2,1,0:T(8,128)(2,1)S(1)}, f32[4,1024,256]{2,1,0:T(8,128)S(1)}) fusion(bf16[4,1024,256]{2,1,0:T(8,128)(2,1)S(1)} %copy-done.12, bf16[1024,1024]{1,0:T(8,128)(2,1)S(1)} %convolution_convert_fusion, f32[1024]{0:T(1024)S(1)} %copy-done.8, f32[1024]{0:T(1024)S(1)} %add_rsqrt_fusion.1), kind=kOutput, calls=%fused_computation.100 | convolution fusion | flops 2152726528 | bytes 10493952 | tf_op jit(solution)/shard_map/rd,pdc->prc/dot_general | solution.py:61
  12.9 0.0 copy-start.13
  12.9 0.0 copy-start.7
  12.9 0.0 copy-start.10
  12.9 0.9 fusion.68
  13.9 0.1 fusion.33
  14.0 0.1 convert_element_type.77
  14.1 0.0 copy-done.7
  14.2 1.2 %reduce-window.6 = f32[2,2,4,128]{3,2,1,0:T(4,128)S(1)} reduce-window(f32[2,2,4,128]{3,2,1,0:T(4,128)S(1)} %reshape.123, f32[]{:T(128)} %constant.15.clone.1), window={size=1x1x1x128 pad=0_0x0_0x0_0x127_0}, to_apply=%region_1.0 | reduce-window | flops 260096 | bytes 16388 | tf_op jit(solution)/shard_map/reduce-window
  15.4 0.2 slice_reduce_fusion
  15.6 0.3 reduce-window.9
  15.9 0.1 broadcast_add_fusion
  16.0 0.1 convert_element_type.74
  16.1 0.0 copy-start.11
  16.2 0.0 copy-start.3
  16.2 0.4 copy.51
  16.6 0.1 slice.40
  16.7 0.1 copy.82
  16.8 0.1 and_convert_fusion
  16.9 0.1 multiply_bitcast_fusion
  16.9 1.4 %fusion.34 = f32[2,2,128,128]{3,2,1,0:T(8,128)} fusion(bf16[2,512,2,128]{1,3,0,2:T(8,128)(2,1)S(1)} %copy.51, bf16[2,512,2,128]{3,2,1,0:T(2,128)(2,1)S(1)} %convert_element_type.74, f32[2,512,2]{1,0,2:T(2,128)S(1)} %multiply_bitcast_fusion), kind=kOutput, calls=%fused_computation.47 | convolution fusion | flops 403177472 | bytes 1318912 | tf_op jit(solution)/shard_map/ujhd,ujhe->hude/dot_general | solution.py:86
  18.4 0.0 all-gather.4.cloned.1.call-update
  18.4 0.0 all-reduce.2.cloned.1.call-start
  18.5 12.8 %all-gather = f32[8,2,1]{1,2,0:T(1,128)S(1)} all-gather(f32[2,2,1]{1,2,0:T(1,128)S(1)} %copy.82), channel_id=2, replica_groups=mesh['grp'=2,'ctx'=4,'head'=4] {'ctx'}, dimensions={0}, use_global_device_ids=true | all-gather | bytes 80 | tf_op jit(solution)/shard_map/all_gather | solution.py:92
  31.3 0.1 copy.79
  31.4 0.5 reshape.129
  32.0 0.5 copy.56
  32.5 1.2 %convert_element_type.75 = bf16[2,512,2,128]{3,2,1,0:T(2,128)(2,1)S(1)} reshape(bf16[1,1024,256]{2,1,0:T(8,128)(2,1)} %get-tuple-element.12) | data formatting | bytes 1048576 | tf_op jit(solution)/shard_map/convert_element_type | solution.py:65
  33.7 0.1 copy.81
  33.8 0.7 copy.84
  34.5 0.1 fusion.29
  34.6 0.7 copy.83
  35.3 0.6 reshape.137
  35.9 0.1 copy.57
  36.1 0.1 reshape.125
  36.1 1.4 %convolution_convert_fusion.1 = bf16[256,1024]{1,0:T(8,128)(2,1)S(1)} fusion(bf16[256,256]{1,0:T(8,128)(2,1)S(1)} %reshape.125, bf16[256,1024]{1,0:T(8,128)(2,1)} %param.16), kind=kOutput, calls=%fused_computation.29 | convolution fusion | flops 134479872 | bytes 1179648 | tf_op jit(solution)/shard_map/dot_general | solution.py:55
  37.5 0.2 fusion.30
  37.7 0.2 fusion.32
  37.9 1.3 %convolution_convert_fusion.2 = bf16[256,256]{1,0:T(8,128)(2,1)S(1)} fusion(bf16[256,1024]{1,0:T(8,128)(2,1)S(1)} %fusion.32, bf16[4,1024,256]{2,1,0:T(8,128)(2,1)} %param.18), kind=kOutput, calls=%fused_computation.31 | convolution fusion | flops 134283264 | bytes 1179648 | tf_op jit(solution)/shard_map/dot_general | solution.py:121
  39.3 0.1 iota_compare_fusion
  39.4 0.7 fusion.40
  40.1 0.2 copy-done.2
  40.3 5.5 %fusion.20 = f32[2,512,2,128]{1,3,2,0:T(8,128)} fusion(f32[2,2,512,512]{3,2,0,1:T(8,128)S(1)} %fusion.40, f32[2,512]{1,0:T(2,128)} %copy-done.6, f32[2,2,512]{2,0,1:T(2,128)S(1)} %get-tuple-element.14, pred[512,512]{1,0:T(8,128)(4,1)S(1)} %iota_compare_fusion, bf16[2,512,2,128]{3,2,1,0:T(2,128)(2,1)S(1)} %copy-done.2), kind=kOutput, calls=%fused_computation.23 | convolution fusion | flops 1615855616 | bytes 6041600 | tf_op jit(solution)/shard_map/huij,ujhd->uihd/dot_general | solution.py:82
  45.8 3.4 %all-gather.4.cloned.1.call-done = f32[8,2,128,128]{3,2,1,0:T(8,128)} async-done(((f32[2,2,128,128]{3,2,1,0:T(8,128)}), f32[8,2,128,128]{3,2,1,0:T(8,128)}) %all-gather.4.cloned.1.call-update) | async-done | bytes 1048592 | tf_op jit(solution)/shard_map/all_gather | solution.py:97
  49.2 1.5 %multiply_reduce_fusion = (bf16[2,2,128,128]{3,2,1,0:T(8,128)(2,1)S(1)}, f32[2,2,128,128]{3,2,1,0:T(8,128)S(1)}) fusion(f32[2,2,4,128,128]{4,3,1,0,2:T(8,128)} %bitcast.62, f32[2,2,4]{1,0,2:T(2,128)S(1)} %copy-done.4, f32[2,2,4]{1,0,2:T(2,128)S(1)} %copy-done.5), kind=kLoop, calls=%fused_computation.43 | loop fusion | flops 917504 | bytes 1441920
  50.7 0.1 copy.78
  50.9 0.2 multiply_reduce_fusion.3
  51.1 0.8 multiply_multiply_fusion
  51.9 0.2 copy.59
  52.1 2.3 %fusion.54 = f32[256,1024]{1,0:T(8,128)} fusion(bf16[256,1024]{1,0:T(8,128)(2,1)} %param.20, f32[32,8,2,128]{3,2,1,0:T(2,128)S(1)} %bitcast.61, bf16[256,1024]{1,0:T(8,128)(2,1)S(1)} %fusion.32, s32[]{:T(128)S(6)} %select_n.24), kind=kOutput, calls=%fused_computation.72 | convolution fusion | flops 134414336 | bytes 1966084 | tf_op jit(solution)/shard_map/dot_general | solution.py:135
  54.4 0.0 all-reduce.2.cloned.1.call-update
  54.5 2.0 %multiply_reduce_fusion.2 = (f32[2,512,2]{1,2,0:T(2,128)S(1)}, f32[2,512,2,128]{1,3,2,0:T(8,128)S(1)}) fusion(f32[2,512,2,128]{1,3,2,0:T(8,128)} %fusion.20, f32[2,512,2]{1,2,0:T(2,128)S(1)} %get-tuple-element.13, bf16[2,512,2,128]{3,2,1,0:T(2,128)(2,1)S(1)} %convert_element_type.75, f32[2,2,128,128]{3,2,1,0:T(8,128)S(1)} %get-tuple-element.9), kind=kOutput, calls=%fused_computation.46 | convolution fusion | flops 403699712 | bytes 2899968 | tf_op jit(solution)/shard_map/uihd,hude->uihe/dot_general | solution.py:110
  56.5 1.1 %multiply_convert_fusion = bf16[2,512,2,128]{1,3,2,0:T(8,128)(2,1)S(1)} fusion(f32[2,512,2,128]{1,3,2,0:T(8,128)S(1)} %copy.56, f32[2,512,2,128]{1,3,2,0:T(8,128)S(1)} %get-tuple-element.18, f32[2,128]{1,0:T(2,128)} %bitcast.70, f32[2,512,2]{1,2,0:T(2,128)S(1)} %add_rsqrt_fusion), kind=kLoop, calls=%fused_computation.45 | loop fusion | flops 2097152 | bytes 2630656 | tf_op jit(solution)/shard_map/convert_element_type | solution.py:118
  57.5 1.0 %copy.60 = bf16[2,512,256]{2,1,0:T(8,128)(2,1)} copy(bf16[2,512,256]{1,2,0:T(8,128)(2,1)S(1)} %bitcast.60) | data formatting | bytes 1048576
  58.5 31.8 %all-reduce.2.cloned.1.call-done = f32[256,1024]{1,0:T(8,128)} async-done(((f32[256,1024]{1,0:T(8,128)}), f32[256,1024]{1,0:T(8,128)}) %all-reduce.2.cloned.1.call-update) | async-done | bytes 1048592 | tf_op jit(solution)/shard_map/psum | solution.py:134
  90.3 1.2 %convolution_bitcast_fusion.3 = f32[64]{0:T(128)S(1)} fusion(bf16[1024,1]{0,1:T(2,128)(2,1)S(1)} %copy-done.9, f32[256,1024]{1,0:T(8,128)} %all-reduce.2.cloned.1.call-done, s32[]{:T(128)S(6)} %select_n.25), kind=kOutput, calls=%fused_computation.37 | convolution fusion | flops 1048576 | bytes 264452 | tf_op jit(solution)/shard_map/dot_general | solution.py:138
  91.5 0.2 reshape.128
  91.6 0.6 copy.61
  (32 shorter events, 0.2 us)
Async XLA Ops:
  7.2 1.0 %copy-start = (bf16[2,512,256]{2,1,0:T(8,128)(2,1)S(1)}, bf16[2,512,256]{2,1,0:T(8,128)(2,1)}, u32[]{:S(2)}) copy-start(bf16[2,512,256]{2,1,0:T(8,128)(2,1)} %param.11) | copy-start | bytes 1572868
  7.2 3.3 %copy-start.12 = (bf16[4,1024,256]{2,1,0:T(8,128)(2,1)S(1)}, bf16[4,1024,256]{2,1,0:T(8,128)(2,1)}, u32[]{:S(2)}) copy-start(bf16[4,1024,256]{2,1,0:T(8,128)(2,1)} %param.18) | copy-start | bytes 6291460
  7.2 3.3 %copy-start.8 = (f32[1024]{0:T(1024)S(1)}, f32[1024]{0:T(1024)}, u32[]{:S(2)}) copy-start(f32[1024]{0:T(1024)} %param.17) | copy-start | bytes 12292
  7.2 42.0 %all-gather.4.cloned.1.call-start = ((), (), s32[]{:S(2)}) async-start(), calls=%async_computation.1 | async-start | bytes 1310720 | tf_op jit(solution)/shard_map/all_gather | solution.py:97
  12.9 1.2 %copy-start.13 = (s32[2]{0:T(128)S(1)}, s32[2]{0:T(128)}, u32[]{:S(2)}) copy-start(s32[2]{0:T(128)} %param.13) | copy-start | bytes 28
  12.9 1.3 %copy-start.7 = (f32[2,2,512]{2,1,0:T(2,128)S(1)}, f32[2,2,512]{2,1,0:T(2,128)}, u32[]{:S(2)}) copy-start(f32[2,2,512]{2,1,0:T(2,128)} %param.14) | copy-start | bytes 24580
  12.9 3.9 %copy-start.10 = (s32[2,512]{1,0:T(2,128)S(1)}, s32[2,512]{1,0:T(2,128)}, u32[]{:S(2)}) copy-start(s32[2,512]{1,0:T(2,128)} %param.12) | copy-start | bytes 12292
  16.1 15.3 %copy-start.1 = (bf16[2,512,2,128]{3,2,1,0:T(2,128)(2,1)}, bf16[2,512,2,128]{3,2,1,0:T(2,128)(2,1)S(1)}, u32[]{:S(2)}) copy-start(bf16[2,512,2,128]{3,2,1,0:T(2,128)(2,1)S(1)} %convert_element_type.74) | copy-start | bytes 1572868
  16.1 19.2 %copy-start.11 = (bf16[1024]{0:T(1024)(128)(2,1)S(1)}, bf16[1024]{0:T(1024)(128)(2,1)}, u32[]{:S(2)}) copy-start(bf16[1024]{0:T(1024)(128)(2,1)} %param.21) | copy-start | bytes 6148
  16.2 19.8 %copy-start.3 = (bf16[2,128,256]{2,1,0:T(8,128)(2,1)S(1)}, bf16[2,128,256]{2,1,0:T(8,128)(2,1)}, u32[]{:S(2)}) copy-start(bf16[2,128,256]{2,1,0:T(8,128)(2,1)} %param.15) | copy-start | bytes 393220
  16.9 1.5 %copy-start.6 = (f32[2,512]{1,0:T(2,128)}, f32[2,512]{1,0:T(2,128)S(1)}, u32[]{:S(2)}) copy-start(f32[2,512]{1,0:T(2,128)S(1)} %and_convert_fusion) | copy-start | bytes 12292
  18.4 71.9 %all-reduce.2.cloned.1.call-start = ((), (), s32[]{:S(2)}) async-start(), calls=%async_computation | async-start | bytes 2097152 | tf_op jit(solution)/shard_map/psum | solution.py:134
  39.3 1.0 %copy-start.2 = (bf16[2,512,2,128]{3,2,1,0:T(2,128)(2,1)S(1)}, bf16[2,512,2,128]{3,2,1,0:T(2,128)(2,1)}, u32[]{:S(2)}) copy-start(bf16[2,512,2,128]{3,2,1,0:T(2,128)(2,1)} %copy-done.1) | copy-start | bytes 1572868
  40.3 8.9 %copy-start.4 = (f32[2,2,4]{1,0,2:T(2,128)S(1)}, f32[2,2,4]{1,0,2:T(2,128)}, u32[]{:S(2)}) copy-start(f32[2,2,4]{1,0,2:T(2,128)} %copy.84) | copy-start | bytes 196
  40.3 8.9 %copy-start.5 = (f32[2,2,4]{1,0,2:T(2,128)S(1)}, f32[2,2,4]{1,0,2:T(2,128)}, u32[]{:S(2)}) copy-start(f32[2,2,4]{1,0,2:T(2,128)} %copy.83) | copy-start | bytes 196
  54.4 35.8 %copy-start.9 = (bf16[1024,1]{0,1:T(2,128)(2,1)S(1)}, bf16[1024,1]{0,1:T(2,128)(2,1)}, u32[]{:S(2)}) copy-start(bf16[1024,1]{0,1:T(2,128)(2,1)} %reshape.137) | copy-start | bytes 6148
Sparse Core Ops, SparseCore 0:
  18.5 30.6 all-gather.3
  54.6 35.6 all-reduce.1
where the time goes:
time: 99.7 us; the launch traced here: 99.1 us
  waiting for transfers between devices  35.2 us (35%)
  matrix products  20.2 us (20%)
  between operations  14.4 us (14%)
  blocking collectives  12.8 us (13%)
  local copies, waits for them, and re-layouts  9.09 us (9%)
  other arithmetic  7.31 us (7%)
    psum x1, waiting for transfers between devices, local(): lax.psum(jnp.dot(candidate_feat, ranker_first, preferred_element_type=jnp...  31.8 us
    all_gather x1, blocking collectives, local(): log_rows = lax.all_gather(span_total[None], 'ctx', axis=0, tiled=True)  12.8 us
    dot_general x1, matrix products, local(): jnp.einsum('huij,ujhd->uihd', scores_local * decay_matrix, value_wide, pr...  5.5 us
    unnamed x35, local copies, waits for them, and re-layouts  5.08 us
    all_gather x1, waiting for transfers between devices, local(): shard_piece = lax.all_gather(local_state[None], 'ctx', axis=0, tiled=True)  3.42 us
    dot_general x1, matrix products, local(): jnp.einsum('rd,pdc->prc', behavior_norm, proj_weight, preferred_element_t...  2.39 us
    dot_general x1, matrix products, local(): jnp.dot(candidate_feat, ranker_first, preferred_element_type=jnp.float32)  2.34 us
  transfers between devices with their start and end apart: 2, of which 2 were waited for; matrix products, arithmetic and copies ran while one was open for 18% of the time, Pallas kernels for 0%

commit v1 on v0

v1 whole, which is shorter than its diff:
```python
import functools

import jax
import jax.numpy as jnp
from jax import lax
from jax.experimental import pallas as pl
from jax.experimental.pallas import tpu as pltpu
from jax.sharding import PartitionSpec as P

DH = 128
EPS = 1e-05
F32 = jnp.float32
BF16 = jnp.bfloat16
ANY = pl.BlockSpec(memory_space=pl.ANY)
HBM = pl.BlockSpec(memory_space=pltpu.HBM)
VMEM = pl.BlockSpec(memory_space=pltpu.VMEM)
SMEM = pl.BlockSpec(memory_space=pltpu.SMEM)


def dot(a, b):
    return jnp.dot(a, b, preferred_element_type=F32)


def dot_nt(a, b):
    return lax.dot_general(a, b, (((1,), (1,)), ((), ())), preferred_element_type=F32)


def dot_tn(a, b):
    return lax.dot_general(a, b, (((0,), (0,)), ((), ())), preferred_element_type=F32)


def scale_rms(values, gain):
    mean_square = jnp.mean(values * values, axis=-1, keepdims=True)
    return values * lax.rsqrt(mean_square + EPS) * gain


def call(kernel, outs, ins, in_specs, out_specs, scratch, name, flops, limit=24):
    total = sum(x.size * x.dtype.itemsize for x in ins)
    return pl.pallas_call(
        kernel,
        out_shape=outs,
        in_specs=in_specs,
        out_specs=out_specs,
        scratch_shapes=scratch,
        name=name,
        compiler_params=pltpu.CompilerParams(vmem_limit_bytes=limit << 20),
        cost_estimate=pl.CostEstimate(flops=flops, bytes_accessed=total, transcendentals=0),
    )(*ins)


def kernel_a(
    users, heads, span, seq_total,
    hist, mask, decay, emb_hbm, win_hbm, gain_ref, proj_hbm,
    norm_out, key_out, value_out, payload, cum_out, valid_out, cum_col_out,
    emb, win, wkv, rows8, sems,
):
    cols = heads * DH
    pairs = heads * users
    block = min(256, span)
    copies = []

    def fetch(src, dst, slot):
        copy = pltpu.make_async_copy(src, dst, sems.at[slot])
        copy.start()
        return copy

    get_win = fetch(win_hbm, win, 0)
    get_emb = [fetch(emb_hbm.at[u], emb.at[u], 1 + u) for u in range(users)]
    get_k = fetch(proj_hbm.at[1], wkv.at[0], 1 + users)
    get_v = fetch(proj_hbm.at[2], wkv.at[1], 2 + users)

    rows8[...] = jnp.zeros_like(rows8)
    for h in range(heads):
        rows8[h * users:(h + 1) * users, :] = decay[h]
    cum = rows8[...]
    lane = lax.broadcasted_iota(jnp.int32, cum.shape, 1)
    step = 1
    while step < span:
        cum = cum + jnp.where(lane >= step, pltpu.roll(cum, step, 1), 0.0)
        step *= 2
    cum_out[...] = cum
    position = lax.axis_index("ctx") * span + lax.broadcasted_iota(jnp.int32, (1, span), 1)
    for u in range(users):
        keep = (position >= seq_total - hist[u]) & (mask[u:u + 1, :] == 1)
        valid_out[u:u + 1, :] = jnp.where(keep, 1.0, 0.0)
    total = cum[:, span - 1:span]
    weight = jnp.exp(total - cum)
    weights = []
    for h in range(heads):
        for u in range(users):
            r = h * users + u
            weights.append(weight[r:r + 1, :] * valid_out[u:u + 1, :])
    for r in range(pairs):
        rows8[r:r + 1, :] = weights[r]
    weight_col = jnp.transpose(rows8[...])
    cum_col_out[...] = jnp.transpose(cum)

    state_rows = pairs * DH
    tail = payload.shape[0] - state_rows
    row_id = lax.broadcasted_iota(jnp.int32, (tail, DH), 0)
    logs = jnp.zeros((tail, DH), F32)
    for r in range(pairs):
        rest = jnp.broadcast_to(total[r:r + 1, :], (tail, DH))
        for t in range(3):
            part = rest.astype(BF16).astype(F32)
            logs = jnp.where(row_id == 3 * r + t, part, logs)
            rest = rest - part
    payload[state_rows:, :] = logs.astype(BF16)

    get_win.wait()
    for u in range(users):
        get_emb[u].wait()
        for b in range(span // block):
            rows = slice(u * span + b * block, u * span + (b + 1) * block)
            raw = dot(emb[u, b * block:(b + 1) * block, :], win[...]).astype(BF16).astype(F32)
            norm_out[rows, :] = scale_rms(raw, gain_ref[...][None, :]).astype(BF16)
        if u == 0:
            get_k.wait()
            get_v.wait()
        for b in range(span // block):
            rows = slice(u * span + b * block, u * span + (b + 1) * block)
            norm = norm_out[rows, :]
            key_out[rows, :] = (dot(norm, wkv[0]) * DH ** -0.5).astype(BF16)
            value_out[rows, :] = dot(norm, wkv[1]).astype(BF16)
        for h in range(heads):
            r = h * users + u
            rows = slice(u * span, (u + 1) * span)
            lanes = slice(h * DH, (h + 1) * DH)
            key = key_out[rows, lanes].astype(F32) * weight_col[:, r:r + 1]
            state = dot_tn(key.astype(BF16), value_out[rows, lanes])
            payload[r * DH:(r + 1) * DH, :] = state.astype(BF16)


def kernel_b(
    users, heads, span,
    norm_ref, key_ref, value_ref, cum, valid, cum_col, proj_hbm,
    cemb, win, gain_ref,
    query_out, gate_out, within_out, cquery_out, own_out,
    wq, wg, cnorm, sems,
):
    cols = heads * DH
    block = min(256, span)
    get_q = pltpu.make_async_copy(proj_hbm.at[0], wq, sems.at[0])
    get_g = pltpu.make_async_copy(proj_hbm.at[3], wg, sems.at[1])
    get_q.start()
    get_g.start()
    cands = cemb.shape[1]
    for u in range(users):
        raw = dot(cemb[u], win[...]).astype(BF16).astype(F32)
        cnorm[u * cands:(u + 1) * cands, :] = scale_rms(raw, gain_ref[...][None, :]).astype(BF16)
    start = pl.multiple_of(lax.axis_index("head") * cols, cols)
    own_out[...] = cnorm[:, pl.ds(start, cols)]
    get_q.wait()
    cquery_out[...] = dot(cnorm[...], wq[...]).astype(BF16)
    get_g.wait()
    for u in range(users):
        for b in range(span // block):
            rows = slice(u * span + b * block, u * span + (b + 1) * block)
            norm = norm_ref[rows, :]
            query_out[rows, :] = dot(norm, wq[...]).astype(BF16)
            gate_out[rows, :] = dot(norm, wg[...]).astype(BF16)
            width = (b + 1) * block
            seen = slice(u * span, u * span + width)
            row_id = b * block + lax.broadcasted_iota(jnp.int32, (block, width), 0)
            col_id = lax.broadcasted_iota(jnp.int32, (block, width), 1)
            keep = (row_id >= col_id) & (valid[u:u + 1, :width] > 0.0)
            for h in range(heads):
                r = h * users + u
                lanes = slice(h * DH, (h + 1) * DH)
                gap = cum_col[b * block:(b + 1) * block, r:r + 1] - cum[r:r + 1, :width]
                pair = dot_nt(query_out[rows, lanes], key_ref[seen, lanes])
                pair = pair * jnp.where(keep, jnp.exp(jnp.minimum(gap, 0.0)), 0.0)
                within_out[rows, lanes] = dot(pair.astype(BF16), value_ref[seen, lanes])


def kernel_c(users, heads, ctx_count, head_count, source, dest, *refs):
    received = refs[:ctx_count]
    cquery, own, gain_ref = refs[ctx_count:ctx_count + 3]
    outs = refs[ctx_count + 3:]
    prefix_out = outs[0]
    feat_outs = outs[1:1 + head_count]
    pieces, feat, sems = outs[1 + head_count:]
    me = lax.axis_index("ctx")
    copies = []
    for k in range(ctx_count):
        copy = pltpu.make_async_copy(received[k], pieces.at[source(me, k, ctx_count)], sems.at[k])
        copy.start()
        copies.append(copy)
    for copy in copies:
        copy.wait()
    pairs = heads * users
    cands = cquery.shape[0] // users
    for u in range(users):
        for h in range(heads):
            r = h * users + u
            rows = pl.ds(r * DH, DH)
            state = pieces[0, r * DH:(r + 1) * DH, :].astype(F32)
            prefix = jnp.zeros((DH, DH), F32)
            for p in range(1, ctx_count):
                prefix = jnp.where(me == p, state, prefix)
                base = pairs * DH + 3 * r
                log = pieces[p, pairs * DH:, :].astype(F32)
                log = jnp.sum(log[3 * r:3 * r + 3, :], axis=0, keepdims=True)
                state = jnp.exp(log) * state + pieces[p, r * DH:(r + 1) * DH, :].astype(F32)
            prefix_out[r * DH:(r + 1) * DH, :] = prefix.astype(BF16)
            lanes = slice(h * DH, (h + 1) * DH)
            crow = slice(u * cands, (u + 1) * cands)
            read = dot(cquery[crow, lanes], state.astype(BF16))
            value = scale_rms(read, gain_ref[lanes][None, :]) + own[crow, lanes].astype(F32)
            feat[crow, lanes] = value.astype(BF16)
    mine = lax.axis_index("head")
    share = cands // head_count
    for k in range(head_count):
        start = pl.multiple_of(dest(mine, k, head_count) * share, share)
        for u in range(users):
            feat_outs[k][u * share:(u + 1) * share, :] = feat[pl.ds(u * cands + start, share), :]


def kernel_d(users, heads, span, within, query, gate, prefix, cum_col, gain_ref, out):
    for u in range(users):
        for h in range(heads):
            r = h * users + u
            rows = slice(u * span, (u + 1) * span)
            lanes = slice(h * DH, (h + 1) * DH)
            carried = dot(query[rows, lanes], prefix[r * DH:(r + 1) * DH, :])
            readout = within[rows, lanes] + carried * jnp.exp(cum_col[:, r:r + 1])
            wide = gate[rows, lanes].astype(F32)
            value = scale_rms(readout, gain_ref[lanes][None, :]) * (wide * jax.nn.sigmoid(wide))
            out[u, :, lanes] = value.astype(BF16)


def kernel_e(users, head_count, *refs):
    feats = refs[:head_count]
    weights = refs[head_count:2 * head_count]
    second, out = refs[2 * head_count:2 * head_count + 2]
    hidden = dot(feats[0][...], weights[0][...])
    for k in range(1, head_count):
        hidden = hidden + dot(feats[k][...], weights[k][...])
    value = hidden * jax.nn.sigmoid(hidden) * second[...].astype(F32)[None, :]
    score = jnp.sum(value, axis=-1, keepdims=True)
    share = score.shape[0] // users
    row_id = lax.broadcasted_iota(jnp.int32, (share, share), 0)
    col_id = lax.broadcasted_iota(jnp.int32, (share, share), 1)
    for u in range(users):
        part = jnp.broadcast_to(score[u * share:(u + 1) * share, :], (share, share))
        out[u:u + 1, :] = jnp.sum(jnp.where(row_id == col_id, part, 0.0), axis=0, keepdims=True)


def is_power(n):
    return n & (n - 1) == 0


def source(index, k, n):
    return index ^ k if is_power(n) else lax.rem(index - k + n, n)


def dest(index, k, n):
    return index ^ k if is_power(n) else lax.rem(index + k, n)


def shift(array, axis, k, n):
    pairs = [(i, i ^ k if is_power(n) else (i + k) % n) for i in range(n)]
    return lax.ppermute(array, axis, pairs)


def local(
    behavior_embed,
    behavior_mask,
    history_len,
    log_decay,
    candidate_embed,
    input_weight,
    input_gain,
    proj_weight,
    output_gain,
    ranker_first,
    ranker_second,
):
    users, span = behavior_mask.shape
    cands = candidate_embed.shape[1]
    width = input_weight.shape[0]
    model = input_weight.shape[1]
    cols = proj_weight.shape[2]
    heads = cols // DH
    pairs = heads * users
    ctx_count = lax.axis_size("ctx")
    head_count = lax.axis_size("head")
    rows = users * span
    share = cands // head_count
    row_pad = -(-pairs // 8) * 8
    tail = -(-3 * pairs // 16) * 16
    payload_rows = pairs * DH + tail
    sds = jax.ShapeDtypeStruct

    norm, key, value, payload, cum, valid, cum_col = call(
        functools.partial(kernel_a, users, heads, span, span * ctx_count),
        (
            sds((rows, model), BF16),
            sds((rows, cols), BF16),
            sds((rows, cols), BF16),
            sds((payload_rows, DH), BF16),
            sds((row_pad, span), F32),
            sds((users, span), F32),
            sds((span, row_pad), F32),
        ),
        (history_len, behavior_mask, log_decay, behavior_embed, input_weight, input_gain,
         proj_weight),
        [SMEM, VMEM, VMEM, HBM, HBM, VMEM, HBM],
        (VMEM,) * 7,
        [
            pltpu.VMEM((users, span, width), BF16),
            pltpu.VMEM((width, model), BF16),
            pltpu.VMEM((2, model, cols), BF16),
            pltpu.VMEM((row_pad, span), F32),
            pltpu.SemaphoreType.DMA((3 + users,)),
        ],
        "features",
        2 * rows * model * (width + 2 * cols),
    )

    pieces = [payload] + [shift(payload, "ctx", k, ctx_count) for k in range(1, ctx_count)]
    forward = is_power(head_count)
    early, _ = lax.optimization_barrier((ranker_first, payload))
    weights = [ranker_first] + [None] * (head_count - 1)
    for k in range(1, head_count):
        if not (forward and k % 2 and k > 1):
            weights[k] = shift(early, "head", k, head_count)

    query, gate, within, cquery, own = call(
        functools.partial(kernel_b, users, heads, span),
        (
            sds((rows, cols), BF16),
            sds((rows, cols), BF16),
            sds((rows, cols), F32),
            sds((users * cands, cols), BF16),
            sds((users * cands, cols), BF16),
        ),
        (norm, key, value, cum, valid, cum_col, proj_weight, candidate_embed, input_weight,
         input_gain),
        [VMEM, VMEM, VMEM, VMEM, VMEM, VMEM, HBM, VMEM, VMEM, VMEM],
        (VMEM,) * 5,
        [
            pltpu.VMEM((model, cols), BF16),
            pltpu.VMEM((model, cols), BF16),
            pltpu.VMEM((users * cands, model), BF16),
            pltpu.SemaphoreType.DMA((2,)),
        ],
        "within",
        2 * rows * model * 2 * cols + 2 * rows * span * cols * 2,
    )

    prefix, *feats = call(
        functools.partial(kernel_c, users, heads, ctx_count, head_count, source, dest),
        (sds((pairs * DH, DH), BF16),) + (sds((users * share, cols), BF16),) * head_count,
        (*pieces, cquery, own, output_gain),
        [ANY] * ctx_count + [VMEM] * 3,
        (VMEM,) * (1 + head_count),
        [
            pltpu.VMEM((ctx_count, payload_rows, DH), BF16),
            pltpu.VMEM((users * cands, cols), BF16),
            pltpu.SemaphoreType.DMA((ctx_count,)),
        ],
        "final",
        2 * users * cands * cols * DH,
    )

    for k in range(1, head_count):
        if weights[k] is None:
            piece, _ = lax.optimization_barrier((weights[k - 1], prefix))
            weights[k] = shift(piece, "head", 1, head_count)
    feats = [feats[0]] + [shift(feats[k], "head", k, head_count) for k in range(1, head_count)]

    history_out = call(
        functools.partial(kernel_d, users, heads, span),
        sds((users, span, cols), BF16),
        (within, query, gate, prefix, cum_col, output_gain),
        [VMEM] * 6,
        VMEM,
        [],
        "carried",
        2 * rows * cols * DH,
    )

    scores = call(
        functools.partial(kernel_e, users, head_count),
        sds((users, share), F32),
        (*feats, *weights, ranker_second),
        [VMEM] * (2 * head_count + 1),
        VMEM,
        [],
        "scores",
        2 * users * share * model * ranker_first.shape[1],
    )
    return (history_out, scores)


def solution(mesh):
    in_specs = (
        P("grp", "ctx", None),
        P("grp", "ctx"),
        P("grp"),
        P("head", "grp", "ctx"),
        P("grp", "ctx", None),
        P(),
        P(),
        P(None, None, "head"),
        P("head"),
        P("head", None),
        P(),
    )
    out_specs = (P("grp", "ctx", "head"), P("grp", ("ctx", "head")))
    return jax.shard_map(local, mesh=mesh, in_specs=in_specs, out_specs=out_specs, check_vma=False)
```

time: 99.7 us -> 37.1 us (0.37)
  waiting for transfers between devices: 35.2 us -> 7.68 us
  matrix products: 20.2 us -> 0 us
  between operations: 14.4 us -> 0.74 us
  blocking collectives: 12.8 us -> 0 us
  Pallas kernels: 0 us -> 12.5 us
  starting transfers between devices: 0.08 us -> 9.43 us
  other arithmetic: 7.31 us -> 0 us
  local copies, waits for them, and re-layouts: 9.09 us -> 6.41 us
    psum x1 -> x0, waiting for transfers between devices: 31.8 us -> none  [local(): lax.psum(jnp.dot(candidate_feat, ranker_first, preferred_element_type=jnp...]
    dot_general x11 -> x0, matrix products: 20.2 us -> none  [the longest x1 5.5 us: local(): jnp.einsum('huij,ujhd->uihd', scores_local * decay_matrix, value_wide, pr...]
    all_gather x1 -> x0, blocking collectives: 12.8 us -> none  [local(): log_rows = lax.all_gather(span_total[None], 'ctx', axis=0, tiled=True)]
    pallas_call x0 -> x5, Pallas kernels: none -> 12.5 us  [call(): pl.pallas_call(kernel, out_shape=outs, in_specs=in_specs, out_specs=out_s...]
    ppermute x0 -> x9, starting transfers between devices: none -> 9.43 us  [shift(): return lax.ppermute(array, axis, pairs)]
    ppermute x0 -> x9, waiting for transfers between devices: none -> 7.68 us  [shift(): return lax.ppermute(array, axis, pairs)]
    all_gather x1 -> x0, waiting for transfers between devices: 3.42 us -> none  [local(): shard_piece = lax.all_gather(local_state[None], 'ctx', axis=0, tiled=True)]
    convert_element_type x6 -> x0, local copies, waits for them, and re-layouts: 2.9 us -> none  [the longest x1 1.17 us: local(): query_rows = projected[0].astype(jnp.bfloat16).reshape(head_shape)]
  transfers between devices with their start and end apart: 2 -> 9, of which waited for: 2 -> 3; matrix products, arithmetic and copies ran while one was open for 18% -> 0% of each run, Pallas kernels for 0% -> 18%
where the time goes in v1:
time: 37.1 us; the launch traced here: 36.8 us
  Pallas kernels  12.5 us (34%)
  starting transfers between devices  9.43 us (25%)
  waiting for transfers between devices  7.68 us (21%)
  local copies, waits for them, and re-layouts  6.41 us (17%)
  between operations  0.74 us (2%)
    pallas_call x5, Pallas kernels, call(): pl.pallas_call(kernel, out_shape=outs, in_specs=in_specs, out_specs=out_s...  12.5 us
    ppermute x9, starting transfers between devices, shift(): return lax.ppermute(array, axis, pairs)  9.43 us
    ppermute x9, waiting for transfers between devices, shift(): return lax.ppermute(array, axis, pairs)  7.68 us
    unnamed x24, local copies, waits for them, and re-layouts  6.41 us
  transfers between devices with their start and end apart: 9, of which 3 were waited for; matrix products, arithmetic and copies ran while one was open for 0% of the time, Pallas kernels for 18%

profile of v1, /device:TPU:0, one launch (start us, length us, event | category | flops | bytes accessed | tf_op | source)
XLA Modules:
  0.0 36.8 jit_solution(379378099296300592)
XLA Ops:
  0.6 0.0 copy-start
  0.6 1.6 %copy-done = bf16[4,1024,256]{2,1,0:T(8,128)(2,1)S(1)} copy-done((bf16[4,1024,256]{2,1,0:T(8,128)(2,1)S(1)}, bf16[4,1024,256]{2,1,0:T(8,128)(2,1)}, u32[]{:S(2)}) %copy-start) | copy-done | bytes 2097176
  2.2 0.0 copy-start.2
  2.2 1.0 %copy-done.2 = bf16[256,1024]{1,0:T(8,128)(2,1)S(1)} copy-done((bf16[256,1024]{1,0:T(8,128)(2,1)S(1)}, bf16[256,1024]{1,0:T(8,128)(2,1)}, u32[]{:S(2)}) %copy-start.2) | copy-done | bytes 524312
  3.3 0.0 copy-start.5
  3.3 0.7 %copy-done.5 = f32[1024]{0:T(1024)S(1)} copy-done((f32[1024]{0:T(1024)S(1)}, f32[1024]{0:T(1024)}, u32[]{:S(2)}) %copy-start.5) | copy-done | bytes 4120
  4.0 0.0 copy-start.8
  4.0 1.0 %copy-done.8 = bf16[2,512,256]{2,1,0:T(8,128)(2,1)S(1)} copy-done((bf16[2,512,256]{2,1,0:T(8,128)(2,1)S(1)}, bf16[2,512,256]{2,1,0:T(8,128)(2,1)}, u32[]{:S(2)}) %copy-start.8) | copy-done | bytes 524312
  5.0 0.0 copy-start.9
  5.0 0.7 %copy-done.9 = f32[2,2,512]{2,1,0:T(2,128)S(1)} copy-done((f32[2,2,512]{2,1,0:T(2,128)S(1)}, f32[2,2,512]{2,1,0:T(2,128)}, u32[]{:S(2)}) %copy-start.9) | copy-done | bytes 8216
  5.7 0.0 copy-start.10
  5.7 0.7 %copy-done.10 = s32[2,512]{1,0:T(2,128)S(1)} copy-done((s32[2,512]{1,0:T(2,128)S(1)}, s32[2,512]{1,0:T(2,128)}, u32[]{:S(2)}) %copy-start.10) | copy-done | bytes 4120
  6.4 0.0 copy-start.11
  6.4 0.7 %copy-done.11 = s32[2]{0:T(128)S(1)} copy-done((s32[2]{0:T(128)S(1)}, s32[2]{0:T(128)}, u32[]{:S(2)}) %copy-start.11) | copy-done | bytes 32
  7.0 0.0 copy-start.3
  7.0 0.0 copy-start.1
  7.0 0.0 copy-start.4
  7.0 4.8 %features.1 = (bf16[1024,1024]{1,0:T(8,128)(2,1)S(1)}, bf16[1024,256]{1,0:T(8,128)(2,1)S(1)}, bf16[1024,256]{1,0:T(8,128)(2,1)S(1)}, bf16[528,128]{1,0:T(8,128)(...) custom-call(s32[2]{0:T(128)S(1)} %copy-done.11, s32[2,512]{1,0:T(2,128)S(1)} %copy-done.10, ...), custom_call_target="tpu_custom_call" | custom-call | flops 1610612736 | bytes 3162120 | tf_op jit(solution)/shard_map/features/pallas_call | solution.py:39
  11.8 0.0 copy-done.3
  11.8 3.0 %collective-permute-start.7 = (bf16[256,1024]{1,0:T(8,128)(2,1)S(1)}, bf16[256,1024]{1,0:T(8,128)(2,1)S(1)}, u32[]{:S(2)}, u32[]{:S(2)}) collective-permute-start(bf16[256,1024]{1,0:T(8,128)(2,1)S(1)} %copy-done.3), channel_id=1, source_target_pairs={{0,2},{1,3},{2,0},{3,1},{4,6},{5,7},{6,4},{7,5},{8,10},{9,11},{10,... | collective-permute-start | bytes 1572872 | tf_op jit(solution)/shard_map/ppermute | solution.py:263
  14.9 3.6 %collective-permute-start.2 = (bf16[528,128]{1,0:T(8,128)(2,1)S(1)}, bf16[528,128]{1,0:T(8,128)(2,1)S(1)}, u32[]{:S(2)}, u32[]{:S(2)}) collective-permute-start(bf16[528,128]{1,0:T(8,128)(2,1)S(1)} %get-tuple-element.30.refs_0_), channel_id=1, source_target_pairs={{0,12},{4,8},{8,4},{12,0},{1,13},{5,9},{9,5},{13,1},{2,14},{6,10},... | collective-permute-start | bytes 405512 | tf_op jit(solution)/shard_map/ppermute | solution.py:263
  18.5 0.0 collective-permute-start.1
  18.5 0.8 %collective-permute-start = (bf16[528,128]{1,0:T(8,128)(2,1)S(1)}, bf16[528,128]{1,0:T(8,128)(2,1)S(1)}, u32[]{:S(2)}, u32[]{:S(2)}) collective-permute-start(bf16[528,128]{1,0:T(8,128)(2,1)S(1)} %get-tuple-element.30.refs_0_), channel_id=1, source_target_pairs={{0,4},{4,0},{8,12},{12,8},{1,5},{5,1},{9,13},{13,9},{2,6},{6,2},{1... | collective-permute-start | bytes 405512 | tf_op jit(solution)/shard_map/ppermute | solution.py:263
  19.3 0.0 collective-permute-start.6
  19.3 0.0 copy-done.1
  19.3 0.0 copy-done.4
  19.3 0.0 copy-start.6
  19.3 3.7 %within.1 = (bf16[1024,256]{1,0:T(8,128)(2,1)S(1)}, bf16[1024,256]{1,0:T(8,128)(2,1)S(1)}, f32[1024,256]{1,0:T(8,128)S(1)}, bf16[256,256]{1,0:T(8,128)(2,1)S(1)}, bf16[256,256]{1,0:T(8,128)(2,1)S(1)}) custom-call(bf16[1024,1024]{1,0:T(8,128)(2,1)S(1)} %get-tuple-element.21.norm_ref, bf16[1024,256]{1,0:T(8,128)(2,1)S(1)} %get-tuple-element.22.key_ref, ...), custom_call_target="tpu_custom_call" | custom-call | flops 1610612736 | bytes 5939200 | tf_op jit(solution)/shard_map/within/pallas_call | solution.py:39
  23.0 0.0 copy-start.7
  23.0 0.2 collective-permute-done.2.refs_3_
  23.2 6.4 %collective-permute-done.1.refs_2_ = bf16[528,128]{1,0:T(8,128)(2,1)S(1)} collective-permute-done((bf16[528,128]{1,0:T(8,128)(2,1)S(1)}, bf16[528,128]{1,0:T(8,128)(2,1)S(1)}, u32[]{:S(2)}, u32[]{:S(2)}) %collective-permute-start.1) | collective-permute-done | bytes 135200 | tf_op jit(solution)/shard_map/ppermute | solution.py:263
  29.6 0.0 collective-permute-done.refs_1_
  29.6 0.0 copy-done.6
  29.6 1.1 %final.1 = (bf16[512,128]{1,0:T(8,128)(2,1)S(1)}, bf16[64,256]{1,0:T(8,128)(2,1)S(1)}, bf16[64,256]{1,0:T(8,128)(2,1)S(1)}, bf16[64,256]{1,0:T(8,128)(2,1)S(1)}, bf16[64,256]{1,0:T(8,128)(2,1)S(1)}) custom-call(bf16[528,128]{1,0:T(8,128)(2,1)S(1)} %get-tuple-element.30.refs_0_, bf16[528,128]{1,0:T(8,128)(2,1)S(1)} %collective-permute-done.refs_1_, ...), custom_call_target="tpu_custom_call" | custom-call | flops 16777216 | bytes 803840 | tf_op jit(solution)/shard_map/final/pallas_call | solution.py:39
  30.8 0.0 collective-permute-done.7.refs_6_
  30.8 0.1 collective-permute-start.8
  30.9 0.5 %collective-permute-start.3 = (bf16[64,256]{1,0:T(8,128)(2,1)S(1)}, bf16[64,256]{1,0:T(8,128)(2,1)S(1)}, u32[]{:S(2)}, u32[]{:S(2)}) collective-permute-start(bf16[64,256]{1,0:T(8,128)(2,1)S(1)} %get-tuple-element.35), channel_id=1, source_target_pairs={{0,1},{1,0},{2,3},{3,2},{4,5},{5,4},{6,7},{7,6},{8,9},{9,8},{10,11... | collective-permute-start | bytes 98312 | tf_op jit(solution)/shard_map/ppermute | solution.py:263
  31.4 0.5 %collective-permute-start.4 = (bf16[64,256]{1,0:T(8,128)(2,1)S(1)}, bf16[64,256]{1,0:T(8,128)(2,1)S(1)}, u32[]{:S(2)}, u32[]{:S(2)}) collective-permute-start(bf16[64,256]{1,0:T(8,128)(2,1)S(1)} %get-tuple-element.36), channel_id=1, source_target_pairs={{0,2},{1,3},{2,0},{3,1},{4,6},{5,7},{6,4},{7,5},{8,10},{9,11},{10,... | collective-permute-start | bytes 98312 | tf_op jit(solution)/shard_map/ppermute | solution.py:263
  31.9 0.9 %collective-permute-start.5 = (bf16[64,256]{1,0:T(8,128)(2,1)S(1)}, bf16[64,256]{1,0:T(8,128)(2,1)S(1)}, u32[]{:S(2)}, u32[]{:S(2)}) collective-permute-start(bf16[64,256]{1,0:T(8,128)(2,1)S(1)} %get-tuple-element.37), channel_id=1, source_target_pairs={{0,3},{1,2},{2,1},{3,0},{4,7},{5,6},{6,5},{7,4},{8,11},{9,10},{10,... | collective-permute-start | bytes 98312 | tf_op jit(solution)/shard_map/ppermute | solution.py:263
  32.8 1.7 %carried.1 = bf16[2,512,256]{2,1,0:T(8,128)(2,1)} custom-call(f32[1024,256]{1,0:T(8,128)S(1)} %get-tuple-element.27.within, bf16[1024,256]{1,0:T(8,128)(2,1)S(1)} %get-tuple-element.28.query, bf16[1024,256]{1,0:T(8,128)(2,1)S(1)} %get-tuple-element.29.gate, bf16[512,128]{1,0:T(8,128)(2,1)S(1)} %get-tuple-element.33.prefix, ...), custom_call_target="tpu_custom_call" | custom-call | flops 67108864 | bytes 2245632 | tf_op jit(solution)/shard_map/carried/pallas_call | solution.py:39
  34.5 0.0 collective-permute-done.3.refs_1_
  34.5 1.1 %collective-permute-done.4.refs_2_ = bf16[64,256]{1,0:T(8,128)(2,1)S(1)} collective-permute-done((bf16[64,256]{1,0:T(8,128)(2,1)S(1)}, bf16[64,256]{1,0:T(8,128)(2,1)S(1)}, u32[]{:S(2)}, u32[]{:S(2)}) %collective-permute-start.4) | collective-permute-done | bytes 32800 | tf_op jit(solution)/shard_map/ppermute | solution.py:263
  35.6 0.0 collective-permute-done.5.refs_3_
  35.6 0.0 collective-permute-done.6.refs_5_
  35.6 0.0 collective-permute-done.8.refs_7_
  35.6 0.0 copy-done.7
  35.6 1.2 %scores.1 = f32[2,32]{1,0:T(2,128)} custom-call(bf16[64,256]{1,0:T(8,128)(2,1)S(1)} %get-tuple-element.34.refs_0_, bf16[64,256]{1,0:T(8,128)(2,1)S(1)} %collective-permute-done.3.refs_1_, bf16[64,256]{1,0:T(8,128)(2,1)S(1)} %collective-permute-done.4.refs_2_, bf16[64,256]{1,0:T(8,128)(2,1)S(1)} %collective-permute-done.5.refs_3_, ...), custom_call_target="tpu_custom_call" | custom-call | flops 134217728 | bytes 2230272 | tf_op jit(solution)/shard_map/scores/pallas_call | solution.py:39
Async XLA Ops:
  0.6 1.6 %copy-start = (bf16[4,1024,256]{2,1,0:T(8,128)(2,1)S(1)}, bf16[4,1024,256]{2,1,0:T(8,128)(2,1)}, u32[]{:S(2)}) copy-start(bf16[4,1024,256]{2,1,0:T(8,128)(2,1)} %proj_hbm.3) | copy-start | bytes 6291460
  2.2 1.0 %copy-start.2 = (bf16[256,1024]{1,0:T(8,128)(2,1)S(1)}, bf16[256,1024]{1,0:T(8,128)(2,1)}, u32[]{:S(2)}) copy-start(bf16[256,1024]{1,0:T(8,128)(2,1)} %win.1) | copy-start | bytes 1572868
  3.3 0.7 %copy-start.5 = (f32[1024]{0:T(1024)S(1)}, f32[1024]{0:T(1024)}, u32[]{:S(2)}) copy-start(f32[1024]{0:T(1024)} %gain_ref.4) | copy-start | bytes 12292
  4.0 1.0 %copy-start.8 = (bf16[2,512,256]{2,1,0:T(8,128)(2,1)S(1)}, bf16[2,512,256]{2,1,0:T(8,128)(2,1)}, u32[]{:S(2)}) copy-start(bf16[2,512,256]{2,1,0:T(8,128)(2,1)} %emb_hbm.1) | copy-start | bytes 1572868
  5.0 0.7 %copy-start.9 = (f32[2,2,512]{2,1,0:T(2,128)S(1)}, f32[2,2,512]{2,1,0:T(2,128)}, u32[]{:S(2)}) copy-start(f32[2,2,512]{2,1,0:T(2,128)} %decay.1) | copy-start | bytes 24580
  5.7 0.7 %copy-start.10 = (s32[2,512]{1,0:T(2,128)S(1)}, s32[2,512]{1,0:T(2,128)}, u32[]{:S(2)}) copy-start(s32[2,512]{1,0:T(2,128)} %mask.1) | copy-start | bytes 12292
  6.4 0.7 %copy-start.11 = (s32[2]{0:T(128)S(1)}, s32[2]{0:T(128)}, u32[]{:S(2)}) copy-start(s32[2]{0:T(128)} %hist.1) | copy-start | bytes 28
  7.0 4.8 %copy-start.3 = (bf16[256,1024]{1,0:T(8,128)(2,1)S(1)}, bf16[256,1024]{1,0:T(8,128)(2,1)}, u32[]{:S(2)}) copy-start(bf16[256,1024]{1,0:T(8,128)(2,1)} %refs_4_.1) | copy-start | bytes 1572868
  7.0 12.2 %copy-start.1 = (bf16[4,1024,256]{2,1,0:T(8,128)(2,1)S(1)}, bf16[4,1024,256]{2,1,0:T(8,128)(2,1)}, u32[]{:S(2)}) copy-start(bf16[4,1024,256]{2,1,0:T(8,128)(2,1)} %proj_hbm.3) | copy-start | bytes 6291460
  7.0 12.2 %copy-start.4 = (bf16[2,128,256]{2,1,0:T(8,128)(2,1)S(1)}, bf16[2,128,256]{2,1,0:T(8,128)(2,1)}, u32[]{:S(2)}) copy-start(bf16[2,128,256]{2,1,0:T(8,128)(2,1)} %cemb.1) | copy-start | bytes 393220
  11.8 18.9 %collective-permute-start.7 = (bf16[256,1024]{1,0:T(8,128)(2,1)S(1)}, bf16[256,1024]{1,0:T(8,128)(2,1)S(1)}, u32[]{:S(2)}, u32[]{:S(2)}) collective-permute-start(bf16[256,1024]{1,0:T(8,128)(2,1)S(1)} %copy-done.3), channel_id=1, source_target_pairs={{0,2},{1,3},{2,0},{3,1},{4,6},{5,7},{6,4},{7,5},{8,10},{9,11},{10,... | collective-permute-start | bytes 1572872 | tf_op jit(solution)/shard_map/ppermute | solution.py:263
  14.9 8.3 %collective-permute-start.2 = (bf16[528,128]{1,0:T(8,128)(2,1)S(1)}, bf16[528,128]{1,0:T(8,128)(2,1)S(1)}, u32[]{:S(2)}, u32[]{:S(2)}) collective-permute-start(bf16[528,128]{1,0:T(8,128)(2,1)S(1)} %get-tuple-element.30.refs_0_), channel_id=1, source_target_pairs={{0,12},{4,8},{8,4},{12,0},{1,13},{5,9},{9,5},{13,1},{2,14},{6,10},... | collective-permute-start | bytes 405512 | tf_op jit(solution)/shard_map/ppermute | solution.py:263
  18.5 11.1 %collective-permute-start.1 = (bf16[528,128]{1,0:T(8,128)(2,1)S(1)}, bf16[528,128]{1,0:T(8,128)(2,1)S(1)}, u32[]{:S(2)}, u32[]{:S(2)}) collective-permute-start(bf16[528,128]{1,0:T(8,128)(2,1)S(1)} %get-tuple-element.30.refs_0_), channel_id=1, source_target_pairs={{0,8},{4,12},{8,0},{12,4},{1,9},{5,13},{9,1},{13,5},{2,10},{6,14},... | collective-permute-start | bytes 405512 | tf_op jit(solution)/shard_map/ppermute | solution.py:263
  18.5 11.1 %collective-permute-start = (bf16[528,128]{1,0:T(8,128)(2,1)S(1)}, bf16[528,128]{1,0:T(8,128)(2,1)S(1)}, u32[]{:S(2)}, u32[]{:S(2)}) collective-permute-start(bf16[528,128]{1,0:T(8,128)(2,1)S(1)} %get-tuple-element.30.refs_0_), channel_id=1, source_target_pairs={{0,4},{4,0},{8,12},{12,8},{1,5},{5,1},{9,13},{13,9},{2,6},{6,2},{1... | collective-permute-start | bytes 405512 | tf_op jit(solution)/shard_map/ppermute | solution.py:263
  19.3 16.3 %collective-permute-start.6 = (bf16[256,1024]{1,0:T(8,128)(2,1)S(1)}, bf16[256,1024]{1,0:T(8,128)(2,1)S(1)}, u32[]{:S(2)}, u32[]{:S(2)}) collective-permute-start(bf16[256,1024]{1,0:T(8,128)(2,1)S(1)} %copy-done.3), channel_id=1, source_target_pairs={{0,1},{1,0},{2,3},{3,2},{4,5},{5,4},{6,7},{7,6},{8,9},{9,8},{10,11... | collective-permute-start | bytes 1572872 | tf_op jit(solution)/shard_map/ppermute | solution.py:263
  19.3 10.3 %copy-start.6 = (f32[256]{0:T(256)S(1)}, f32[256]{0:T(256)}, u32[]{:S(2)}) copy-start(f32[256]{0:T(256)} %gain_ref.5) | copy-start | bytes 3076
  23.0 12.6 %copy-start.7 = (bf16[1024]{0:T(1024)(128)(2,1)S(1)}, bf16[1024]{0:T(1024)(128)(2,1)}, u32[]{:S(2)}) copy-start(bf16[1024]{0:T(1024)(128)(2,1)} %refs_8_.1) | copy-start | bytes 6148
  30.8 4.8 %collective-permute-start.8 = (bf16[256,1024]{1,0:T(8,128)(2,1)S(1)}, bf16[256,1024]{1,0:T(8,128)(2,1)S(1)}, u32[]{:S(2)}, u32[]{:S(2)}) collective-permute-start(bf16[256,1024]{1,0:T(8,128)(2,1)S(1)} %collective-permute-done.7.refs_6_), channel_id=1, source_target_pairs={{0,1},{1,0},{2,3},{3,2},{4,5},{5,4},{6,7},{7,6},{8,9},{9,8},{10,11... | collective-permute-start | bytes 1572872 | tf_op jit(solution)/shard_map/ppermute | solution.py:263
  30.9 3.6 %collective-permute-start.3 = (bf16[64,256]{1,0:T(8,128)(2,1)S(1)}, bf16[64,256]{1,0:T(8,128)(2,1)S(1)}, u32[]{:S(2)}, u32[]{:S(2)}) collective-permute-start(bf16[64,256]{1,0:T(8,128)(2,1)S(1)} %get-tuple-element.35), channel_id=1, source_target_pairs={{0,1},{1,0},{2,3},{3,2},{4,5},{5,4},{6,7},{7,6},{8,9},{9,8},{10,11... | collective-permute-start | bytes 98312 | tf_op jit(solution)/shard_map/ppermute | solution.py:263
  31.4 4.2 %collective-permute-start.4 = (bf16[64,256]{1,0:T(8,128)(2,1)S(1)}, bf16[64,256]{1,0:T(8,128)(2,1)S(1)}, u32[]{:S(2)}, u32[]{:S(2)}) collective-permute-start(bf16[64,256]{1,0:T(8,128)(2,1)S(1)} %get-tuple-element.36), channel_id=1, source_target_pairs={{0,2},{1,3},{2,0},{3,1},{4,6},{5,7},{6,4},{7,5},{8,10},{9,11},{10,... | collective-permute-start | bytes 98312 | tf_op jit(solution)/shard_map/ppermute | solution.py:263
  31.9 3.7 %collective-permute-start.5 = (bf16[64,256]{1,0:T(8,128)(2,1)S(1)}, bf16[64,256]{1,0:T(8,128)(2,1)S(1)}, u32[]{:S(2)}, u32[]{:S(2)}) collective-permute-start(bf16[64,256]{1,0:T(8,128)(2,1)S(1)} %get-tuple-element.37), channel_id=1, source_target_pairs={{0,3},{1,2},{2,1},{3,0},{4,7},{5,6},{6,5},{7,4},{8,11},{9,10},{10,... | collective-permute-start | bytes 98312 | tf_op jit(solution)/shard_map/ppermute | solution.py:263
